TPU v7x, 32 devices: a whole 2x2x4 slice. The times are simulated.
32 devices in a mesh: replica: 8 (over y, x, core), shard: 4 (over z).
Axes of the slice: x: 2, y: 2, z: 4, core: 2. Of those that a mesh axis runs over, the one named last changes fastest.
Arguments:
- inputs: bfloat16 [4096, 2048], P(('replica', 'shard')), may hold values from -6 to 6
- lengths: int32 [8, 8], P('replica'), may hold values from 1 to 256, 512 in all within a row
- ln_gain: float32 [2048], replicated, may hold values from 0.5 to 1.5
- ln_bias: float32 [2048], replicated, may hold values from -3 to 3
- qkv_weight: bfloat16 [2048, 3, 2048], P(None, None, 'shard'), may hold values from -0.125 to 0.125
- qkv_bias: float32 [3, 2048], P(None, 'shard'), may hold values from -3 to 3
- out_weight: bfloat16 [2048, 2048], P('shard'), may hold values from -0.5 to 0.5
- fc1_weight: bfloat16 [2048, 8192], P(None, 'shard'), may hold values from -0.125 to 0.125
- fc1_bias: float32 [8192], P('shard'), may hold values from -3 to 3
- fc2_weight: bfloat16 [8192, 2048], P('shard'), may hold values from -0.0625 to 0.0625
- out_bias: float32 [2048], replicated, may hold values from -3 to 3
- cotangent: bfloat16 [4096, 2048], P(('replica', 'shard')), may hold values from -6 to 6
Outputs:
- output: bfloat16 [4096, 2048], P(('replica', 'shard'))
- input_grad: float32 [4096, 2048], P(('replica', 'shard'))
- ln_gain_grad: float32 [2048], P('shard')
- ln_bias_grad: float32 [2048], P('shard')
- qkv_weight_grad: float32 [2048, 3, 2048], P(None, None, 'shard')
- qkv_bias_grad: float32 [3, 2048], P(None, 'shard')
- out_weight_grad: float32 [2048, 2048], P('shard')
- fc1_weight_grad: float32 [2048, 8192], P(None, 'shard')
- fc1_bias_grad: float32 [8192], P('shard')
- fc2_weight_grad: float32 [8192, 2048], P('shard')
- out_bias_grad: float32 [2048], replicated
Inputs may be any that keep to these rules, and one draw needn't show every extreme that they name: Row g of lengths holds the lengths of the 8 sequences of replica group g in order; they add up to 512, and the longest is 256.
All inputs are finite; a program needn't handle non-finite values.
Results may differ from a plain program's by a relative error of at most 0.011.
Values may be sent and summed in bfloat16 or wider, within the bound.
No kernel may reach another device: no remote copies, remote signals or barrier semaphores. Data moves between devices by JAX's collectives and lax.ppermute only.
A program may use at most 320 MiB of HBM per device.

v0:
```python
import math
import jax
import jax.numpy as jnp
from jax import lax
from jax.sharding import PartitionSpec as P

HD = 64
ROT = 32


def normalize(x_float):
    mean_row = jnp.mean(x_float, axis=-1, keepdims=True)
    centred = x_float - mean_row
    inv_std = lax.rsqrt(jnp.mean(centred * centred, axis=-1, keepdims=True) + 1e-05)
    return (centred * inv_std, inv_std)


def positions(length_row, count):
    ends = jnp.cumsum(length_row, dtype=jnp.int32)
    row_ids = jnp.arange(count, dtype=jnp.int32)
    passed = (row_ids[:, None] >= ends[None, :]).astype(jnp.int32)
    segment = jnp.sum(passed, axis=1, dtype=jnp.int32)
    begin = jnp.sum(passed * length_row[None, :], axis=1, dtype=jnp.int32)
    offset = (row_ids - begin).astype(jnp.float32)
    freq_ids = jnp.arange(ROT // 2, dtype=jnp.float32)
    inverse = jnp.exp(freq_ids * (-2.0 * math.log(10000.0) / ROT))
    angle_rows = offset[:, None] * inverse[None, :]
    return (segment, row_ids, jnp.cos(angle_rows), jnp.sin(angle_rows))


def rotate(values, cosine, sine):
    half = ROT // 2
    first = values[..., :half]
    second = values[..., half:ROT]
    cos_b = cosine[:, None, :]
    sin_b = sine[:, None, :]
    return jnp.concatenate(
        [first * cos_b - second * sin_b, second * cos_b + first * sin_b, values[..., ROT:]], axis=-1
    )


def unrotate(values, cosine, sine):
    half = ROT // 2
    first = values[..., :half]
    second = values[..., half:ROT]
    cos_b = cosine[:, None, :]
    sin_b = sine[:, None, :]
    return jnp.concatenate(
        [first * cos_b + second * sin_b, second * cos_b - first * sin_b, values[..., ROT:]], axis=-1
    )


def gelu_tanh(inner):
    coef = math.sqrt(2.0 / math.pi)
    return 0.5 * inner * (1.0 + jnp.tanh(coef * (inner + 0.044715 * inner * inner * inner)))


def gelu_slope(inner):
    coef = math.sqrt(2.0 / math.pi)
    tangent = jnp.tanh(coef * (inner + 0.044715 * inner * inner * inner))
    return 0.5 * (1.0 + tangent) + 0.5 * inner * (1.0 - tangent * tangent) * coef * (
        1.0 + 3.0 * 0.044715 * inner * inner
    )


def allowed_mask(seg_block, row_block, segment, row_ids):
    return (seg_block[:, None] == segment[None, :]) & (row_ids[None, :] <= row_block[:, None])


def attend(query, keys, values, segment, row_ids):
    count, heads = (query.shape[0], query.shape[1])
    block = min(512, count)
    blocks = count // block

    def per_block(entry):
        q_block, seg_block, row_block = entry
        scores = (
            jnp.einsum("qhd,khd->hqk", q_block, keys, preferred_element_type=jnp.float32) * 0.125
        )
        allowed = allowed_mask(seg_block, row_block, segment, row_ids)[None]
        log_total = jnp.log(jnp.sum(jnp.where(allowed, jnp.exp(scores), 0.0), axis=-1))
        probs = jnp.where(allowed, jnp.exp(scores - log_total[..., None]), 0.0).astype(jnp.bfloat16)
        context = jnp.einsum(
            "hqk,khd->qhd", probs, values, preferred_element_type=jnp.float32
        ).astype(jnp.bfloat16)
        return (context, log_total)

    contexts, totals = lax.map(
        per_block,
        (
            query.reshape(blocks, block, heads, HD),
            segment.reshape(blocks, block),
            row_ids.reshape(blocks, block),
        ),
    )
    return (contexts.reshape(count, heads, HD), totals)


def attend_back(query, keys, values, totals, grad_context, segment, row_ids):
    count, heads = (query.shape[0], query.shape[1])
    block = min(512, count)
    blocks = count // block

    def per_block(carry, entry):
        grad_keys, grad_values = carry
        q_block, g_block, total_block, seg_block, row_block = entry
        scores = (
            jnp.einsum("qhd,khd->hqk", q_block, keys, preferred_element_type=jnp.float32) * 0.125
        )
        allowed = allowed_mask(seg_block, row_block, segment, row_ids)[None]
        probs = jnp.where(allowed, jnp.exp(scores - total_block[..., None]), 0.0)
        probs_low = probs.astype(jnp.bfloat16)
        grad_probs = jnp.einsum("qhd,khd->hqk", g_block, values, preferred_element_type=jnp.float32)
        grad_scores = (
            probs * (grad_probs - jnp.sum(probs * grad_probs, axis=-1, keepdims=True)) * 0.125
        ).astype(jnp.bfloat16)
        grad_query = jnp.einsum(
            "hqk,khd->qhd", grad_scores, keys, preferred_element_type=jnp.float32
        )
        grad_keys = grad_keys + jnp.einsum(
            "hqk,qhd->khd", grad_scores, q_block, preferred_element_type=jnp.float32
        )
        grad_values = grad_values + jnp.einsum(
            "hqk,qhd->khd", probs_low, g_block, preferred_element_type=jnp.float32
        )
        return ((grad_keys, grad_values), grad_query)

    zeros = jnp.zeros(keys.shape, jnp.float32)
    stacked = (
        query.reshape(blocks, block, heads, HD),
        grad_context.reshape(blocks, block, heads, HD),
        totals,
        segment.reshape(blocks, block),
        row_ids.reshape(blocks, block),
    )
    (grad_keys, grad_values), grad_queries = lax.scan(per_block, (zeros, zeros), stacked)
    return (grad_queries.reshape(count, heads, HD), grad_keys, grad_values)


def shards(
    inputs,
    lengths,
    ln_gain,
    ln_bias,
    qkv_weight,
    qkv_bias,
    out_weight,
    fc1_weight,
    fc1_bias,
    fc2_weight,
    out_bias,
    cotangent,
):
    rows_dev, width = inputs.shape
    qkv_flat = qkv_weight.reshape(width, -1)
    qkv_cols = qkv_flat.shape[1]
    heads_local = qkv_cols // (3 * HD)
    x_float = inputs.astype(jnp.float32)
    x_hat, inv_std = normalize(x_float)
    normed = (x_hat * ln_gain + ln_bias).astype(jnp.bfloat16)
    normed_full = lax.all_gather(normed, "shard", axis=0, tiled=True)
    qkv_pre = jnp.dot(normed_full, qkv_flat, preferred_element_type=jnp.float32)
    pre = jnp.dot(normed_full, fc1_weight, preferred_element_type=jnp.float32)
    group_rows = qkv_pre.shape[0]
    qkv = (qkv_pre + qkv_bias.reshape(-1)).reshape(group_rows, 3, heads_local, HD)
    segment, row_ids, cosine, sine = positions(lengths[0], group_rows)
    query = rotate(qkv[:, 0], cosine, sine).astype(jnp.bfloat16)
    keys = rotate(qkv[:, 1], cosine, sine).astype(jnp.bfloat16)
    values = qkv[:, 2].astype(jnp.bfloat16)
    context, totals = attend(query, keys, values, segment, row_ids)
    context_flat = context.reshape(group_rows, -1)
    pre = pre + fc1_bias
    hidden = gelu_tanh(pre).astype(jnp.bfloat16)
    mixed = lax.psum_scatter(
        jnp.dot(context_flat, out_weight, preferred_element_type=jnp.float32)
        + jnp.dot(hidden, fc2_weight, preferred_element_type=jnp.float32),
        "shard",
        scatter_dimension=0,
        tiled=True,
    )
    output = (x_float + mixed + out_bias).astype(jnp.bfloat16)
    cot_full = lax.all_gather(cotangent, "shard", axis=0, tiled=True)
    grad_out_w = jnp.dot(context_flat.T, cot_full, preferred_element_type=jnp.float32)
    grad_fc2 = jnp.dot(hidden.T, cot_full, preferred_element_type=jnp.float32)
    grad_out_b = jnp.sum(cot_full, axis=0, dtype=jnp.float32)
    grad_pre = jnp.dot(cot_full, fc2_weight.T, preferred_element_type=jnp.float32) * gelu_slope(pre)
    grad_fc1_b = jnp.sum(grad_pre, axis=0)
    grad_pre_low = grad_pre.astype(jnp.bfloat16)
    grad_fc1 = jnp.dot(normed_full.T, grad_pre_low, preferred_element_type=jnp.float32)
    grad_context = (
        jnp.dot(cot_full, out_weight.T, preferred_element_type=jnp.float32)
        .astype(jnp.bfloat16)
        .reshape(group_rows, heads_local, HD)
    )
    grad_query, grad_keys, grad_values = attend_back(
        query, keys, values, totals, grad_context, segment, row_ids
    )
    grad_qkv = jnp.stack(
        [unrotate(grad_query, cosine, sine), unrotate(grad_keys, cosine, sine), grad_values], axis=1
    ).reshape(group_rows, qkv_cols)
    grad_qkv_b = jnp.sum(grad_qkv, axis=0).reshape(qkv_bias.shape)
    grad_qkv_low = grad_qkv.astype(jnp.bfloat16)
    grad_qkv_w = jnp.dot(normed_full.T, grad_qkv_low, preferred_element_type=jnp.float32).reshape(
        qkv_weight.shape
    )
    grad_normed = lax.psum_scatter(
        jnp.dot(grad_qkv_low, qkv_flat.T, preferred_element_type=jnp.float32)
        + jnp.dot(grad_pre_low, fc1_weight.T, preferred_element_type=jnp.float32),
        "shard",
        scatter_dimension=0,
        tiled=True,
    )
    norm_parts = jnp.stack(
        [jnp.sum(grad_normed * x_hat, axis=0), jnp.sum(grad_normed, axis=0)], axis=0
    )
    norm_shares = lax.psum_scatter(norm_parts, "shard", scatter_dimension=1, tiled=True)
    scaled = grad_normed * ln_gain
    input_grad = cotangent.astype(jnp.float32) + inv_std * (
        scaled
        - jnp.mean(scaled, axis=-1, keepdims=True)
        - x_hat * jnp.mean(scaled * x_hat, axis=-1, keepdims=True)
    )
    grad_qkv_b, grad_fc1_b, grad_out_b, norm_shares = lax.psum(
        (grad_qkv_b, grad_fc1_b, grad_out_b, norm_shares), "replica"
    )
    low_sums = lax.psum(
        tuple((g.astype(jnp.bfloat16) for g in (grad_qkv_w, grad_out_w, grad_fc1, grad_fc2))),
        "replica",
    )
    grad_qkv_w, grad_out_w, grad_fc1, grad_fc2 = (g.astype(jnp.float32) for g in low_sums)
    return (
        output,
        input_grad,
        norm_shares[0],
        norm_shares[1],
        grad_qkv_w,
        grad_qkv_b,
        grad_out_w,
        grad_fc1,
        grad_fc1_b,
        grad_fc2,
        grad_out_b,
    )


def solution(mesh):
    placed = (
        P(("replica", "shard"), None),
        P("replica", None),
        P(),
        P(),
        P(None, None, "shard"),
        P(None, "shard"),
        P("shard", None),
        P(None, "shard"),
        P("shard"),
        P("shard", None),
        P(),
        P(("replica", "shard"), None),
    )
    return jax.shard_map(
        shards,
        mesh=mesh,
        in_specs=placed,
        out_specs=(
            P(("replica", "shard"), None),
            P(("replica", "shard"), None),
            P("shard"),
            P("shard"),
            P(None, None, "shard"),
            P(None, "shard"),
            P("shard", None),
            P(None, "shard"),
            P("shard"),
            P("shard", None),
            P(),
        ),
        check_vma=False,
    )
```

profile of v0, /device:TPU:0, one launch (start us, length us, event | category | flops | bytes accessed | tf_op | source)
XLA Modules:
  0.0 733.0 jit_solution(2110832071851290796)
XLA Ops:
  13.7 8.8 %copy.45 = bf16[2048,3,512]{0,2,1:T(8,128)(2,1)} copy(bf16[2048,3,512]{2,0,1:T(8,128)(2,1)} %param.16) | data formatting | bytes 12582912 | tf_op args[4]
  23.2 37.5 %all-gather.3.cloned.1.call-done = bf16[512,2048]{1,0:T(8,128)(2,1)} async-done(((bf16[128,2048]{1,0:T(8,128)(2,1)}), bf16[512,2048]{1,0:T(8,128)(2,1)}) %all-gather.3.cloned.1.call-update) | async-done | bytes 2097168 | tf_op jit(solution)/shard_map/all_gather | solution.py:161
  60.7 8.5 %convolution_add_fusion.1 = f32[512,1536]{1,0:T(8,128)} fusion(bf16[512,2048]{1,0:T(8,128)(2,1)} %all-gather.3.cloned.1.call-done, bf16[2048,1536]{0,1:T(8,128)(2,1)} %bitcast.69, f32[1536]{0:T(1024)S(1)} %add.117), kind=kOutput, calls=%fused_computation.31 | convolution fusion | flops 3222011904 | bytes 11540480 | tf_op jit(solution)/shard_map/dot_general | solution.py:162
  76.5 30.3 %all-gather.5.cloned.1.call-done = bf16[512,2048]{1,0:T(8,128)(2,1)} async-done(((bf16[128,2048]{1,0:T(8,128)(2,1)}), bf16[512,2048]{1,0:T(8,128)(2,1)}) %all-gather.5.cloned.1.call-update) | async-done | bytes 2097168 | tf_op jit(solution)/shard_map/all_gather | solution.py:182
  109.7 6.1 fusion.68
  116.8 9.1 %fusion.3 = f32[8,512,512]{1,2,0:T(8,128)} fusion(pred[512,512]{0,1:T(8,128)(4,1)S(1)} %fusion.64, bf16[512,8,32]{0,2,1:T(8,128)(2,1)} %slice.113, bf16[512,8,16]{0,2,1:T(8,128)(2,1)} %get-tuple-element.108, bf16[512,8,16]{0,2,1:T(8,128)(2,1)} %get-tuple-element.109, bf16[512,8,32]{0,2,1:T(8,128)(2,1)} %slice.114, ...), kind=kOutput, calls=%fused_computation.4 | convolution fusion | flops 553652736 | bytes 9699328 | tf_op jit(solution)/shard_map/while/body/eval_jaxpr/reduce_sum | solution.py:81
  125.9 5.0 fusion.34
  130.9 14.6 %fusion.37 = f32[512,8,64]{0,2,1:T(8,128)} fusion(f32[8,512,512]{1,2,0:T(8,128)} %fusion.3, f32[8,512,512]{1,2,0:T(8,128)} %fusion.68, bf16[512,8,32]{0,2,1:T(8,128)(2,1)} %slice.113, bf16[512,8,16]{0,2,1:T(8,128)(2,1)} %get-tuple-element.108, bf16[512,8,16]{0,2,1:T(8,128)(2,1)} %get-tuple-element.109), kind=kOutput, calls=%fused_computation.46 | convolution fusion | flops 280498688 | bytes 18350080 | tf_op jit(solution)/shard_map/while/body/eval_jaxpr/hqk,khd->qhd/dot_general | solution.py:117
  145.5 13.9 %fusion.40 = f32[512,8,64]{0,2,1:T(8,128)} fusion(f32[8,512,512]{1,2,0:T(8,128)} %fusion.3, f32[8,512,512]{1,2,0:T(8,128)} %fusion.68, bf16[512,8,32]{0,2,1:T(8,128)(2,1)S(1)} %copy-done.13, bf16[512,8,16]{0,2,1:T(8,128)(2,1)} %get-tuple-element.101, bf16[512,8,16]{0,2,1:T(8,128)(2,1)} %get-tuple-element.100), kind=kOutput, calls=%fused_computation.47 | convolution fusion | flops 280498688 | bytes 18350080 | tf_op jit(solution)/shard_map/while/body/eval_jaxpr/hqk,qhd->khd/dot_general | solution.py:120
  169.2 6.1 fusion.80
  175.2 12.5 %fusion.79 = (f32[2048]{0:T(1024)S(1)}, bf16[512,2048]{1,0:T(8,128)(2,1)}) fusion(f32[512,2048]{1,0:T(8,128)} %fusion.80, f32[2048]{0:T(1024)S(1)} %copy-done.19, bf16[512,2048]{1,0:T(8,128)(2,1)S(1)} %copy-done.10, bf16[2048,2048]{1,0:T(8,128)(2,1)} %param.21), kind=kOutput, calls=%fused_computation.111 | convolution fusion | flops 4316985344 | bytes 16793600 | tf_op jit(solution)/shard_map/dot_general | solution.py:186
  187.8 7.7 %convolution_add_fusion.2 = f32[512,2048]{1,0:T(8,128)} fusion(f32[512,2048]{1,0:T(8,128)S(1)} %copy-done.20, bf16[2048,2048]{1,0:T(8,128)(2,1)S(1)} %bitcast.89, bf16[512,2048]{1,0:T(8,128)(2,1)} %get-tuple-element.115), kind=kOutput, calls=%fused_computation.33 | convolution fusion | flops 4296015872 | bytes 18874368 | tf_op jit(solution)/shard_map/dot_general | solution.py:208
  200.5 8.0 %fusion.77 = f32[512,2048]{1,0:T(8,128)S(1)} fusion(bf16[2048,2048]{1,0:T(8,128)(2,1)} %param.21, f32[512,2048]{1,0:T(8,128)S(1)} %copy-done.21, f32[2048]{0:T(1024)S(1)} %copy-done.19), kind=kOutput, calls=%fused_computation.109 | convolution fusion | flops 4305453056 | bytes 16785408 | tf_op jit(solution)/shard_map/dot_general | solution.py:176
  212.2 8.4 %convolution_convert_fusion.2 = bf16[2048,3,512]{2,0,1:T(8,128)(2,1)} fusion(bf16[3,512,512]{2,1,0:T(8,128)(2,1)} %bitcast.79, bf16[512,2048]{1,0:T(8,128)(2,1)} %all-gather.3.cloned.1.call-done), kind=kOutput, calls=%fused_computation.16 | convolution fusion | flops 3224371200 | bytes 9961472 | tf_op jit(solution)/shard_map/dot_general | solution.py:203
  220.6 6.8 convolution_convert_fusion.1
  227.5 7.6 %convolution_convert_fusion = bf16[2048,2048]{1,0:T(8,128)(2,1)} fusion(bf16[512,2048]{1,0:T(8,128)(2,1)S(1)} %copy-done.11, f32[512,2048]{1,0:T(8,128)S(1)} %copy-done.22, f32[2048]{0:T(1024)S(1)} %copy-done.19), kind=kOutput, calls=%fused_computation.11 | convolution fusion | flops 4309647360 | bytes 14688256 | tf_op jit(solution)/shard_map/dot_general | solution.py:184
  235.1 36.2 %reduce-scatter.8.cloned.1.call-done = f32[128,2048]{1,0:T(8,128)} async-done(((f32[512,2048]{1,0:T(8,128)}), f32[128,2048]{1,0:T(8,128)}) %reduce-scatter.8.cloned.1.call-update) | async-done | bytes 1048592 | tf_op jit(solution)/shard_map/reduce_scatter | solution.py:206
  283.5 67.2 %reduce-scatter.6.cloned.1.call-done = f32[128,2048]{1,0:T(8,128)} async-done(((f32[512,2048]{1,0:T(8,128)}), f32[128,2048]{1,0:T(8,128)}) %reduce-scatter.6.cloned.1.call-update) | async-done | bytes 1048592 | tf_op jit(solution)/shard_map/reduce_scatter | solution.py:174
  354.0 26.7 %reduce-scatter.10.cloned.1.call-done = f32[512,2]{1,0:T(8,128)} async-done(((f32[2048,2]{1,0:T(8,128)}), f32[512,2]{1,0:T(8,128)}) %reduce-scatter.10.cloned.1.call-update) | async-done | bytes 4112
  381.8 26.0 %all-reduce = (f32[2,512]{1,0:T(2,128)S(1)}, f32[3,512]{1,0:T(4,128)}, f32[2048]{0:T(1024)}, f32[2048]{0:T(1024)}) all-reduce(f32[2,512]{1,0:T(2,128)S(1)} %copy.59, f32[3,512]{1,0:T(4,128)S(1)} %reshape.220, f32[2048]{0:T(1024)S(1)} %get-tuple-element.114, ...), channel_id=1, replica_groups=mesh['replica'=8,'shard'=4] {'replica'}, use_global_device_ids=true, to_apply=%region_14.15 | all-reduce | flops 6656 | bytes 53248 | tf_op jit(solution)/shard_map/psum | solution.py:223
  408.3 283.3 %all-reduce.4.cloned.1.call-done = (bf16[2048,3,512]{2,0,1:T(8,128)(2,1)}, bf16[512,2048]{1,0:T(8,128)(2,1)}, bf16[2048,2048]{1,0:T(8,128)(2,1)}, bf16[2048,2048]{1,0:T(8,128)(2,1)}) async-done(((bf16[2048,3,512]{2,0,1:T(8,128)(2,1)}, bf16[512,2048]{1,0:T(8,128)(2,1)}, bf16[2048,2048]{1,0:T(8,128)(2,1)}, bf16[2048,2048]{1,0:T(8,128)(2,1)}), (bf16[2048,3,512]{2,0,1:T(8,128)(2,1)}, ...) | async-done | bytes 25165840 | tf_op jit(solution)/shard_map/psum | solution.py:226
  695.9 6.6 convert_element_type.111
  702.5 11.7 %convert_element_type.115 = f32[2048,2048]{1,0:T(8,128)} convert(bf16[2048,2048]{1,0:T(8,128)(2,1)} %get-tuple-element.92) | non-fusion elementwise | flops 4194304 | bytes 25165824 | tf_op jit(solution)/shard_map/convert_element_type | solution.py:230
  714.2 11.7 %convert_element_type.117 = f32[2048,2048]{1,0:T(8,128)} convert(bf16[2048,2048]{1,0:T(8,128)(2,1)} %get-tuple-element.93) | non-fusion elementwise | flops 4194304 | bytes 25165824 | tf_op jit(solution)/shard_map/convert_element_type | solution.py:230
  (111 shorter events, 58.0 us)
Async XLA Ops:
  7.2 99.6 %copy-start = (bf16[512,2048]{1,0:T(8,128)(2,1)S(1)}, bf16[512,2048]{1,0:T(8,128)(2,1)}, u32[]{:S(2)}) copy-start(bf16[512,2048]{1,0:T(8,128)(2,1)} %param.18) | copy-start | bytes 6291460
  7.2 53.5 %all-gather.3.cloned.1.call-start = ((), (), s32[]{:S(2)}) async-start(), calls=%async_computation.3 | async-start | bytes 2621440 | tf_op jit(solution)/shard_map/all_gather | solution.py:161
  12.2 94.6 %all-gather.5.cloned.1.call-start = ((), (), s32[]{:S(2)}) async-start(), calls=%async_computation.5 | async-start | bytes 2621440 | tf_op jit(solution)/shard_map/all_gather | solution.py:182
  13.0 258.3 %reduce-scatter.8.cloned.1.call-start = ((), (), s32[]{:S(2)}) async-start(), calls=%async_computation.6 | async-start | bytes 5242880 | tf_op jit(solution)/shard_map/reduce_scatter | solution.py:206
  13.7 8.8 %copy-start.16 = (s32[1,8]{1,0:T(1,128)S(1)}, s32[1,8]{1,0:T(1,128)}, u32[]{:S(2)}) copy-start(s32[1,8]{1,0:T(1,128)} %param.13) | copy-start | bytes 100
  109.7 6.1 copy-start.8
  109.7 6.1 copy-start.7
  130.8 30.3 %copy-start.2 = (f32[512,1,8,64]{0,3,2,1:T(8,128)}, f32[512,1,8,64]{0,3,2,1:T(8,128)S(1)}, u32[]{:S(2)}) copy-start(f32[512,1,8,64]{0,3,2,1:T(8,128)S(1)} %fusion.34) | copy-start | bytes 3145732
  130.9 14.6 %copy-start.13 = (bf16[512,8,32]{0,2,1:T(8,128)(2,1)S(1)}, bf16[512,8,32]{0,2,1:T(8,128)(2,1)}, u32[]{:S(2)}) copy-start(bf16[512,8,32]{0,2,1:T(8,128)(2,1)} %slice.114) | copy-start | bytes 786436
  161.2 7.9 %slice-start.4 = ((s8[8388608]{0:T(1024)(128)(4,1)}), s8[4194304]{0:T(1024)(128)(4,1)S(1)}, s32[]{:S(2)}) async-start(s8[8388608]{0:T(1024)(128)(4,1)} %bitcast.88), calls=%async_computation.13 | async-start | bytes 8388608
  162.5 6.6 copy-start.12
  169.1 6.1 copy-start.10
  175.2 12.6 %copy-start.20 = (f32[512,2048]{1,0:T(8,128)S(1)}, f32[512,2048]{1,0:T(8,128)}, u32[]{:S(2)}) copy-start(f32[512,2048]{1,0:T(8,128)} %fusion.81) | copy-start | bytes 12582916
  195.5 155.2 %reduce-scatter.6.cloned.1.call-start = ((), (), s32[]{:S(2)}) async-start(), calls=%async_computation.4 | async-start | bytes 5242880 | tf_op jit(solution)/shard_map/reduce_scatter | solution.py:174
  211.9 168.8 %reduce-scatter.10.cloned.1.call-start = ((), (), s32[]{:S(2)}) async-start(), calls=%async_computation.7 | async-start | bytes 1310720
  212.2 8.4 %copy-start.18 = (bf16[512,2048]{1,0:T(8,128)(2,1)S(1)}, bf16[512,2048]{1,0:T(8,128)(2,1)}, u32[]{:S(2)}) copy-start(bf16[512,2048]{1,0:T(8,128)(2,1)} %all-gather.3.cloned.1.call-done) | copy-start | bytes 6291460
  212.2 8.4 %copy-start.23 = (bf16[512,2048]{1,0:T(8,128)(2,1)S(1)}, bf16[512,2048]{1,0:T(8,128)(2,1)}, u32[]{:S(2)}) copy-start(bf16[512,2048]{1,0:T(8,128)(2,1)} %get-tuple-element.115) | copy-start | bytes 6291460
  220.6 6.9 copy-start.11
  220.6 6.9 copy-start.22
  227.5 43.8 %copy-start.1 = (bf16[128,2048]{1,0:T(8,128)(2,1)S(1)}, bf16[128,2048]{1,0:T(8,128)(2,1)}, u32[]{:S(2)}) copy-start(bf16[128,2048]{1,0:T(8,128)(2,1)} %param.12) | copy-start | bytes 1572868
  227.5 43.8 %copy-start.14 = (f32[2048]{0:T(1024)S(1)}, f32[2048]{0:T(1024)}, u32[]{:S(2)}) copy-start(f32[2048]{0:T(1024)} %param.14) | copy-start | bytes 24580
  274.3 417.3 %all-reduce.4.cloned.1.call-start = ((), (), s32[]{:S(2)}) async-start(), calls=%async_computation.8 | async-start | bytes 50331648 | tf_op jit(solution)/shard_map/psum | solution.py:226
  278.6 72.2 %copy-start.9 = (bf16[128,2048]{1,0:T(8,128)(2,1)S(1)}, bf16[128,2048]{1,0:T(8,128)(2,1)}, u32[]{:S(2)}) copy-start(bf16[128,2048]{1,0:T(8,128)(2,1)} %param.23) | copy-start | bytes 1572868
  278.6 72.1 %copy-start.15 = (f32[2048]{0:T(1024)S(1)}, f32[2048]{0:T(1024)}, u32[]{:S(2)}) copy-start(f32[2048]{0:T(1024)} %param.22) | copy-start | bytes 24580
  (12 other events, 38.0 us)
Sparse Core Ops, SparseCore 0:
  12.3 48.3 all-gather.2
  62.3 44.4 all-gather.4
  195.6 75.5 reduce-scatter.7
  273.4 77.2 reduce-scatter.5
  352.9 27.7 reduce-scatter.9
  385.9 305.6 all-reduce.3
where the time goes:
time: 741 us; the launch traced here: 733 us
  waiting for transfers between devices  482 us (65%)
  matrix products  134 us (18%)
  other arithmetic  52.6 us (7%)
  blocking collectives  26 us (4%)
  local copies, waits for them, and re-layouts  22.7 us (3%)
  between operations  14.7 us (2%)
    psum x1, waiting for transfers between devices, shards(): lax.psum(tuple((g.astype(jnp.bfloat16) for g in (grad_qkv_w, grad_out_w,...  283 us
    reduce_scatter x1, waiting for transfers between devices, shards(): lax.psum_scatter(jnp.dot(context_flat, out_weight, preferred_element_type...  67.2 us
    all_gather x1, waiting for transfers between devices, shards(): normed_full = lax.all_gather(normed, 'shard', axis=0, tiled=True)  37.5 us
    reduce_scatter x1, waiting for transfers between devices, shards(): lax.psum_scatter(jnp.dot(grad_qkv_low, qkv_flat.T, preferred_element_type...  36.2 us
    convert_element_type x4, other arithmetic, shards(): g.astype(jnp.float32)  34.2 us
    all_gather x1, waiting for transfers between devices, shards(): cot_full = lax.all_gather(cotangent, 'shard', axis=0, tiled=True)  30.3 us
    unnamed x7, waiting for transfers between devices  27.5 us
    psum x1, blocking collectives, shards(): lax.psum((grad_qkv_b, grad_fc1_b, grad_out_b, norm_shares), 'replica')  26 us
  transfers between devices with their start and end apart: 6, of which 6 were waited for; matrix products, arithmetic and copies ran while one was open for 11% of the time, Pallas kernels for 0%

commit v1 on v0

--- a/solution.py
+++ b/solution.py
@@ -158,7 +158,13 @@
     x_float = inputs.astype(jnp.float32)
     x_hat, inv_std = normalize(x_float)
     normed = (x_hat * ln_gain + ln_bias).astype(jnp.bfloat16)
-    normed_full = lax.all_gather(normed, "shard", axis=0, tiled=True)
+    size = lax.axis_size("shard")
+    held, pieces = (normed, [normed])
+    for _ in range(size - 1):
+        held = lax.ppermute(held, "shard", [(i, (i + 1) % size) for i in range(size)])
+        pieces.insert(0, held)
+    line = jnp.concatenate(pieces, axis=0)
+    normed_full = jnp.roll(line, (lax.axis_index("shard") + 1) * normed.shape[0], axis=0)
     qkv_pre = jnp.dot(normed_full, qkv_flat, preferred_element_type=jnp.float32)
     pre = jnp.dot(normed_full, fc1_weight, preferred_element_type=jnp.float32)
     group_rows = qkv_pre.shape[0]

time: 741 us -> 729 us (0.984)
  waiting for transfers between devices: 482 us -> 469 us
    ppermute x0 -> x3, waiting for transfers between devices: none -> 46.4 us  [shards(): lax.ppermute(held, 'shard', [(i, (i + 1) % size) for i in range(size)])]
    all_gather x1 -> x0, waiting for transfers between devices: 37.5 us -> none  [shards(): normed_full = lax.all_gather(normed, 'shard', axis=0, tiled=True)]
    all_gather x1, waiting for transfers between devices: 30.3 us -> 0.01 us  [shards(): cot_full = lax.all_gather(cotangent, 'shard', axis=0, tiled=True)]
    reduce_scatter x1, waiting for transfers between devices: 36.2 us -> 44.8 us  [shards(): lax.psum_scatter(jnp.dot(grad_qkv_low, qkv_flat.T, preferred_element_type...]
    unnamed x59 -> x69, local copies, waits for them, and re-layouts: 14.4 us -> 20.3 us
    unnamed x7 -> x6, waiting for transfers between devices: 27.5 us -> 26.8 us
  transfers between devices with their start and end apart: 6 -> 8, of which waited for: 6 -> 7; matrix products, arithmetic and copies ran while one was open for 11% -> 14% of each run, Pallas kernels for 0% -> 0%
where the time goes in v1:
time: 729 us; the launch traced here: 723 us
  waiting for transfers between devices  469 us (64%)
  matrix products  130 us (18%)
  other arithmetic  53.2 us (7%)
  local copies, waits for them, and re-layouts  27.6 us (4%)
  blocking collectives  26 us (4%)
  between operations  14.5 us (2%)
    psum x1, waiting for transfers between devices, shards(): lax.psum(tuple((g.astype(jnp.bfloat16) for g in (grad_qkv_w, grad_out_w,...  283 us
    reduce_scatter x1, waiting for transfers between devices, shards(): lax.psum_scatter(jnp.dot(context_flat, out_weight, preferred_element_type...  67.5 us
    ppermute x3, waiting for transfers between devices, shards(): lax.ppermute(held, 'shard', [(i, (i + 1) % size) for i in range(size)])  46.4 us
    reduce_scatter x1, waiting for transfers between devices, shards(): lax.psum_scatter(jnp.dot(grad_qkv_low, qkv_flat.T, preferred_element_type...  44.8 us
    convert_element_type x4, other arithmetic, shards(): g.astype(jnp.float32)  34.2 us
    unnamed x6, waiting for transfers between devices  26.8 us
    psum x1, blocking collectives, shards(): lax.psum((grad_qkv_b, grad_fc1_b, grad_out_b, norm_shares), 'replica')  26 us
    unnamed x69, local copies, waits for them, and re-layouts  20.3 us
  transfers between devices with their start and end apart: 8, of which 7 were waited for; matrix products, arithmetic and copies ran while one was open for 14% of the time, Pallas kernels for 0%

profile of v1, /device:TPU:0, one launch (start us, length us, event | category | flops | bytes accessed | tf_op | source)
XLA Modules:
  0.0 723.2 jit_solution(7400975058335595648)
XLA Ops:
  14.5 13.9 %collective-permute-done = bf16[128,2048]{1,0:T(8,128)(2,1)S(1)} collective-permute-done((bf16[128,2048]{1,0:T(8,128)(2,1)S(1)}, bf16[128,2048]{1,0:T(8,128)(2,1)S(1)}, u32[]{:S(2)}, u32[]{:S(2)}) %collective-permute-start) | collective-permute-done | bytes 524320 | tf_op jit(solution)/shard_map/ppermute | solution.py:164
  30.1 8.9 %copy.45 = bf16[2048,3,512]{0,2,1:T(8,128)(2,1)} copy(bf16[2048,3,512]{2,0,1:T(8,128)(2,1)} %param.16) | data formatting | bytes 12582912 | tf_op args[4]
  39.1 6.3 collective-permute-done.1
  45.9 26.1 %collective-permute-done.2 = bf16[128,2048]{1,0:T(8,128)(2,1)S(1)} collective-permute-done((bf16[128,2048]{1,0:T(8,128)(2,1)}, bf16[128,2048]{1,0:T(8,128)(2,1)S(1)}, u32[]{:S(2)}, u32[]{:S(2)}) %collective-permute-start.2) | collective-permute-done | bytes 524320 | tf_op jit(solution)/shard_map/ppermute | solution.py:164
  77.2 5.1 convolution_add_fusion.1
  89.2 8.2 %fusion.3 = f32[8,512,512]{1,2,0:T(8,128)} fusion(pred[512,512]{0,1:T(8,128)(4,1)S(1)} %fusion.69, bf16[512,8,32]{0,2,1:T(8,128)(2,1)S(1)} %slice.113, bf16[512,8,16]{0,2,1:T(8,128)(2,1)} %get-tuple-element.108, bf16[512,8,16]{0,2,1:T(8,128)(2,1)} %get-tuple-element.109, bf16[512,8,32]{0,2,1:T(8,128)(2,1)S(1)} %slice.114, ...), kind=kOutput, calls=%fused_computation.4 | convolution fusion | flops 553652736 | bytes 9699328 | tf_op jit(solution)/shard_map/while/body/eval_jaxpr/reduce_sum | solution.py:81
  97.4 10.5 %fusion.45 = f32[512,2048]{1,0:T(8,128)} fusion(bf16[2048,2048]{1,0:T(8,128)(2,1)} %param.19, bf16[1024,2048]{1,0:T(8,128)(2,1)} %copy-done.15, s32[]{:T(128)S(6)} %select_n.25), kind=kOutput, calls=%fused_computation.50 | convolution fusion | flops 4294967296 | bytes 14680068 | tf_op jit(solution)/shard_map/dot_general | solution.py:169
  110.9 6.1 fusion.73
  119.4 14.2 %fusion.37 = f32[512,8,64]{0,2,1:T(8,128)} fusion(f32[8,512,512]{1,2,0:T(8,128)} %fusion.3, f32[8,512,512]{1,2,0:T(8,128)} %fusion.73, bf16[512,8,32]{0,2,1:T(8,128)(2,1)S(1)} %slice.113, bf16[512,8,16]{0,2,1:T(8,128)(2,1)} %get-tuple-element.108, bf16[512,8,16]{0,2,1:T(8,128)(2,1)} %get-tuple-element.109), kind=kOutput, calls=%fused_computation.46 | convolution fusion | flops 280498688 | bytes 18350080 | tf_op jit(solution)/shard_map/while/body/eval_jaxpr/hqk,khd->qhd/dot_general | solution.py:117
  133.6 13.0 %fusion.40 = f32[512,8,64]{0,2,1:T(8,128)} fusion(f32[8,512,512]{1,2,0:T(8,128)} %fusion.3, f32[8,512,512]{1,2,0:T(8,128)} %fusion.73, bf16[512,8,32]{0,2,1:T(8,128)(2,1)S(1)} %slice.114, bf16[512,8,16]{0,2,1:T(8,128)(2,1)S(1)} %copy-done.13, bf16[512,8,16]{0,2,1:T(8,128)(2,1)S(1)} %copy-done.12), kind=kOutput, calls=%fused_computation.47 | convolution fusion | flops 280498688 | bytes 18350080 | tf_op jit(solution)/shard_map/while/body/eval_jaxpr/hqk,qhd->khd/dot_general | solution.py:120
  157.0 11.4 %fusion.88 = (f32[2048]{0:T(1024)S(1)}, bf16[512,2048]{1,0:T(8,128)(2,1)S(1)}) fusion(f32[512,2048]{1,0:T(8,128)} %fusion.45, f32[2048]{0:T(1024)S(1)} %copy-done.19, bf16[512,2048]{1,0:T(8,128)(2,1)S(1)} %copy-done.8, bf16[2048,2048]{1,0:T(8,128)(2,1)} %param.21), kind=kOutput, calls=%fused_computation.128 | convolution fusion | flops 4316985344 | bytes 16793600 | tf_op jit(solution)/shard_map/dot_general | solution.py:192
  169.7 7.7 %convolution_add_fusion.2 = f32[512,2048]{1,0:T(8,128)} fusion(f32[512,2048]{1,0:T(8,128)} %fusion.89, bf16[2048,2048]{1,0:T(8,128)(2,1)S(1)} %bitcast.88, bf16[512,2048]{1,0:T(8,128)(2,1)S(1)} %get-tuple-element.115), kind=kOutput, calls=%fused_computation.33 | convolution fusion | flops 4296015872 | bytes 18874368 | tf_op jit(solution)/shard_map/dot_general | solution.py:214
  182.4 7.9 %fusion.86 = f32[512,2048]{1,0:T(8,128)S(1)} fusion(bf16[2048,2048]{1,0:T(8,128)(2,1)} %param.21, f32[512,2048]{1,0:T(8,128)S(1)} %copy-done.20, f32[2048]{0:T(1024)S(1)} %copy-done.19), kind=kOutput, calls=%fused_computation.126 | convolution fusion | flops 4305453056 | bytes 16785408 | tf_op jit(solution)/shard_map/dot_general | solution.py:182
  193.8 8.4 %convolution_convert_fusion.2 = bf16[2048,3,512]{2,0,1:T(8,128)(2,1)} fusion(bf16[3,512,512]{2,1,0:T(8,128)(2,1)} %bitcast.78, bf16[1024,2048]{1,0:T(8,128)(2,1)} %copy-done.15, s32[]{:T(128)S(6)} %select_n.25), kind=kOutput, calls=%fused_computation.16 | convolution fusion | flops 3224371200 | bytes 9961476 | tf_op jit(solution)/shard_map/dot_general | solution.py:209
  202.3 7.1 convolution_convert_fusion.1
  209.4 7.5 %convolution_convert_fusion = bf16[2048,2048]{1,0:T(8,128)(2,1)} fusion(bf16[512,2048]{1,0:T(8,128)(2,1)S(1)} %copy-done.9, f32[512,2048]{1,0:T(8,128)S(1)} %copy-done.21, f32[2048]{0:T(1024)S(1)} %copy-done.19), kind=kOutput, calls=%fused_computation.11 | convolution fusion | flops 4309647360 | bytes 14688256 | tf_op jit(solution)/shard_map/dot_general | solution.py:190
  216.9 44.8 %reduce-scatter.8.cloned.1.call-done = f32[128,2048]{1,0:T(8,128)} async-done(((f32[512,2048]{1,0:T(8,128)}), f32[128,2048]{1,0:T(8,128)}) %reduce-scatter.8.cloned.1.call-update) | async-done | bytes 1048592 | tf_op jit(solution)/shard_map/reduce_scatter | solution.py:212
  273.9 67.5 %reduce-scatter.6.cloned.1.call-done = f32[128,2048]{1,0:T(8,128)} async-done(((f32[512,2048]{1,0:T(8,128)}), f32[128,2048]{1,0:T(8,128)}) %reduce-scatter.6.cloned.1.call-update) | async-done | bytes 1048592 | tf_op jit(solution)/shard_map/reduce_scatter | solution.py:180
  344.6 26.7 %reduce-scatter.10.cloned.1.call-done = f32[512,2]{1,0:T(8,128)} async-done(((f32[2048,2]{1,0:T(8,128)}), f32[512,2]{1,0:T(8,128)}) %reduce-scatter.10.cloned.1.call-update) | async-done | bytes 4112
  372.3 26.0 %all-reduce = (f32[2,512]{1,0:T(2,128)S(1)}, f32[3,512]{1,0:T(4,128)}, f32[2048]{0:T(1024)}, f32[2048]{0:T(1024)}) all-reduce(f32[2,512]{1,0:T(2,128)S(1)} %copy.59, f32[3,512]{1,0:T(4,128)S(1)} %reshape.220, f32[2048]{0:T(1024)S(1)} %get-tuple-element.114, ...), channel_id=1, replica_groups=mesh['replica'=8,'shard'=4] {'replica'}, use_global_device_ids=true, to_apply=%region_14.15 | all-reduce | flops 6656 | bytes 53248 | tf_op jit(solution)/shard_map/psum | solution.py:229
  398.9 283.3 %all-reduce.4.cloned.1.call-done = (bf16[2048,3,512]{2,0,1:T(8,128)(2,1)}, bf16[512,2048]{1,0:T(8,128)(2,1)}, bf16[2048,2048]{1,0:T(8,128)(2,1)}, bf16[2048,2048]{1,0:T(8,128)(2,1)}) async-done(((bf16[2048,3,512]{2,0,1:T(8,128)(2,1)}, bf16[512,2048]{1,0:T(8,128)(2,1)}, bf16[2048,2048]{1,0:T(8,128)(2,1)}, bf16[2048,2048]{1,0:T(8,128)(2,1)}), (bf16[2048,3,512]{2,0,1:T(8,128)(2,1)}, ...) | async-done | bytes 25165840 | tf_op jit(solution)/shard_map/psum | solution.py:232
  686.5 6.6 convert_element_type.111
  693.1 11.7 %convert_element_type.115 = f32[2048,2048]{1,0:T(8,128)} convert(bf16[2048,2048]{1,0:T(8,128)(2,1)} %get-tuple-element.92) | non-fusion elementwise | flops 4194304 | bytes 25165824 | tf_op jit(solution)/shard_map/convert_element_type | solution.py:236
  704.7 11.7 %convert_element_type.117 = f32[2048,2048]{1,0:T(8,128)} convert(bf16[2048,2048]{1,0:T(8,128)(2,1)} %get-tuple-element.93) | non-fusion elementwise | flops 4194304 | bytes 25165824 | tf_op jit(solution)/shard_map/convert_element_type | solution.py:236
  (127 shorter events, 68.1 us)
Async XLA Ops:
  7.2 100.7 %copy-start = (bf16[512,2048]{1,0:T(8,128)(2,1)S(1)}, bf16[512,2048]{1,0:T(8,128)(2,1)}, u32[]{:S(2)}) copy-start(bf16[512,2048]{1,0:T(8,128)(2,1)} %param.18) | copy-start | bytes 6291460
  7.2 100.7 %all-gather.2.cloned.1.call-start = ((), (), s32[]{:S(2)}) async-start(), calls=%async_computation.4 | async-start | bytes 2621440 | tf_op jit(solution)/shard_map/all_gather | solution.py:188
  11.4 17.1 %collective-permute-start = (bf16[128,2048]{1,0:T(8,128)(2,1)S(1)}, bf16[128,2048]{1,0:T(8,128)(2,1)S(1)}, u32[]{:S(2)}, u32[]{:S(2)}) collective-permute-start(bf16[128,2048]{1,0:T(8,128)(2,1)S(1)} %fusion.58), channel_id=1, source_target_pairs={{0,1},{1,2},{2,3},{3,0},{4,5},{5,6},{6,7},{7,4},{8,9},{9,10},{10,1... | collective-permute-start | bytes 1572872 | tf_op jit(solution)/shard_map/ppermute | solution.py:164
  28.4 17.0 %collective-permute-start.1 = (bf16[128,2048]{1,0:T(8,128)(2,1)S(1)}, bf16[128,2048]{1,0:T(8,128)(2,1)}, u32[]{:S(2)}, u32[]{:S(2)}) collective-permute-start(bf16[128,2048]{1,0:T(8,128)(2,1)S(1)} %collective-permute-done), channel_id=1, source_target_pairs={{0,1},{1,2},{2,3},{3,0},{4,5},{5,6},{6,7},{7,4},{8,9},{9,10},{10,1... | collective-permute-start | bytes 1572872 | tf_op jit(solution)/shard_map/ppermute | solution.py:164
  28.5 233.2 %reduce-scatter.8.cloned.1.call-start = ((), (), s32[]{:S(2)}) async-start(), calls=%async_computation.5 | async-start | bytes 5242880 | tf_op jit(solution)/shard_map/reduce_scatter | solution.py:212
  30.1 8.9 %copy-start.18 = (s32[1,8]{1,0:T(1,128)S(1)}, s32[1,8]{1,0:T(1,128)}, u32[]{:S(2)}) copy-start(s32[1,8]{1,0:T(1,128)} %param.13) | copy-start | bytes 100
  30.1 43.1 %copy-start.1 = (bf16[128,2048]{1,0:T(8,128)(2,1)S(1)}, bf16[128,2048]{1,0:T(8,128)(2,1)}, u32[]{:S(2)}) copy-start(bf16[128,2048]{1,0:T(8,128)(2,1)} %param.12) | copy-start | bytes 1572868
  30.1 43.1 %copy-start.11 = (f32[2048]{0:T(1024)S(1)}, f32[2048]{0:T(1024)}, u32[]{:S(2)}) copy-start(f32[2048]{0:T(1024)} %param.14) | copy-start | bytes 24580
  30.1 43.1 %copy-start.14 = (f32[2048]{0:T(1024)S(1)}, f32[2048]{0:T(1024)}, u32[]{:S(2)}) copy-start(f32[2048]{0:T(1024)} %param.15) | copy-start | bytes 24580
  45.4 26.6 %collective-permute-start.2 = (bf16[128,2048]{1,0:T(8,128)(2,1)}, bf16[128,2048]{1,0:T(8,128)(2,1)S(1)}, u32[]{:S(2)}, u32[]{:S(2)}) collective-permute-start(bf16[128,2048]{1,0:T(8,128)(2,1)} %collective-permute-done.1), channel_id=1, source_target_pairs={{0,1},{1,2},{2,3},{3,0},{4,5},{5,6},{6,7},{7,4},{8,9},{9,10},{10,1... | collective-permute-start | bytes 1572872 | tf_op jit(solution)/shard_map/ppermute | solution.py:164
  45.9 31.3 %copy-start.5 = (bf16[2048,3,512]{0,2,1:T(8,128)(2,1)S(1)}, bf16[2048,3,512]{0,2,1:T(8,128)(2,1)}, u32[]{:S(2)}) copy-start(bf16[2048,3,512]{0,2,1:T(8,128)(2,1)} %copy.45) | copy-start | bytes 18874372
  107.9 9.1 %slice-start = ((s8[8388608]{0:T(1024)(128)(4,1)}), s8[4194304]{0:T(1024)(128)(4,1)S(1)}, s32[]{:S(2)}) async-start(s8[8388608]{0:T(1024)(128)(4,1)} %bitcast.63), calls=%async_computation.8 | async-start | bytes 8388608
  119.4 14.2 %copy-start.12 = (bf16[512,8,16]{0,2,1:T(8,128)(2,1)S(1)}, bf16[512,8,16]{0,2,1:T(8,128)(2,1)}, u32[]{:S(2)}) copy-start(bf16[512,8,16]{0,2,1:T(8,128)(2,1)} %get-tuple-element.100) | copy-start | bytes 393220
  119.4 14.2 %copy-start.13 = (bf16[512,8,16]{0,2,1:T(8,128)(2,1)S(1)}, bf16[512,8,16]{0,2,1:T(8,128)(2,1)}, u32[]{:S(2)}) copy-start(bf16[512,8,16]{0,2,1:T(8,128)(2,1)} %get-tuple-element.101) | copy-start | bytes 393220
  149.3 7.6 %copy-start.10 = (bf16[512,3,8,64]{0,3,2,1:T(8,128)(2,1)}, bf16[512,3,8,64]{0,3,2,1:T(8,128)(2,1)S(1)}, u32[]{:S(2)}) copy-start(bf16[512,3,8,64]{0,3,2,1:T(8,128)(2,1)S(1)} %fusion.28) | copy-start | bytes 4718596
  151.9 17.8 %slice-start.6 = ((s8[8388608]{0:T(1024)(128)(4,1)}), s8[4194304]{0:T(1024)(128)(4,1)S(1)}, s32[]{:S(2)}) async-start(s8[8388608]{0:T(1024)(128)(4,1)} %bitcast.87), calls=%async_computation.14 | async-start | bytes 8388608
  157.0 12.7 %slice-start.7 = ((s8[8388608]{0:T(1024)(128)(4,1)}), s8[4194304]{0:T(1024)(128)(4,1)S(1)}, s32[]{:S(2)}) async-start(s8[8388608]{0:T(1024)(128)(4,1)} %bitcast.87), calls=%async_computation.15 | async-start | bytes 8388608
  177.4 163.9 %reduce-scatter.6.cloned.1.call-start = ((), (), s32[]{:S(2)}) async-start(), calls=%async_computation.3 | async-start | bytes 5242880 | tf_op jit(solution)/shard_map/reduce_scatter | solution.py:180
  193.8 177.5 %reduce-scatter.10.cloned.1.call-start = ((), (), s32[]{:S(2)}) async-start(), calls=%async_computation.6 | async-start | bytes 1310720
  193.8 8.4 %copy-start.16 = (bf16[1024,2048]{1,0:T(8,128)(2,1)S(1)}, bf16[1024,2048]{1,0:T(8,128)(2,1)}, u32[]{:S(2)}) copy-start(bf16[1024,2048]{1,0:T(8,128)(2,1)} %copy-done.15) | copy-start | bytes 12582916
  193.8 8.4 %copy-start.23 = (bf16[512,2048]{1,0:T(8,128)(2,1)S(1)}, bf16[512,2048]{1,0:T(8,128)(2,1)}, u32[]{:S(2)}) copy-start(bf16[512,2048]{1,0:T(8,128)(2,1)} %copy-done.22) | copy-start | bytes 6291460
  264.8 417.4 %all-reduce.4.cloned.1.call-start = ((), (), s32[]{:S(2)}) async-start(), calls=%async_computation.7 | async-start | bytes 50331648 | tf_op jit(solution)/shard_map/psum | solution.py:232
  269.0 72.3 %copy-start.7 = (bf16[128,2048]{1,0:T(8,128)(2,1)S(1)}, bf16[128,2048]{1,0:T(8,128)(2,1)}, u32[]{:S(2)}) copy-start(bf16[128,2048]{1,0:T(8,128)(2,1)} %param.23) | copy-start | bytes 1572868
  269.0 72.3 %copy-start.17 = (f32[2048]{0:T(1024)S(1)}, f32[2048]{0:T(1024)}, u32[]{:S(2)}) copy-start(f32[2048]{0:T(1024)} %param.22) | copy-start | bytes 24580
  (16 other events, 58.0 us)
Sparse Core Ops, SparseCore 0:
  28.6 60.2 all-gather.1
  177.6 84.0 reduce-scatter.7
  264.0 77.2 reduce-scatter.5
  343.5 27.7 reduce-scatter.9
  376.5 305.6 all-reduce.3
